TPU v7x, 32 devices: a whole 2x2x4 slice. The times are simulated.
32 devices in a mesh: groups: 2 (over y), rank: 16 (over z, x, core).
Axes of the slice: x: 2, y: 2, z: 4, core: 2. Of those that a mesh axis runs over, the one named last changes fastest.
Arguments:
- pool: bfloat16 [512, 1024], P(('groups', 'rank')), parts along dimension 0, may hold values from -6 to 6
- kv_cache: bfloat16 [128, 4, 64, 256], P(('groups', 'rank')), parts along dimension 0
- w_qu: bfloat16 [1024, 1024], replicated, may hold values from -0.1875 to 0.1875
- w_out: bfloat16 [512, 1024], replicated, may hold values from -0.25 to 0.25
- norm_gain: float32 [512], replicated, may hold values from 0.1 to 1.9
- cand_ids: int32 [8, 2048], P('groups'), parts along dimension 0, may hold values from 0 to 255
- ranker: int32 [4], replicated, may hold values from 0 to 3, each once
- hist_blocks: int32 [8], P('groups'), parts along dimension 0, may hold values from 4 to 16, as said below
- cache_slot: int32 [8, 16], P('groups'), parts along dimension 0, may hold values from 0 to 63, as said below
Outputs:
- ranked: bfloat16 [16384, 1024], P(('groups', 'rank')), parts along dimension 0
There are 2 independent parts, one for each index of `groups`. A program takes and returns all parts, laid end to end along the dimension named above; an argument that names none is the same for every part. Nothing has to cross between parts.
Inputs may be any that keep to these rules, and one draw needn't show every extreme that they name: Block b of user u (b < 16) is held in slot cache_slot[u, b], which lies on device cache_slot[u, b] // 4 of the rank axis. Each slot holds exactly one pair (u, b); the 16 blocks of one user lie on 16 different devices. `ranker`: each ranking group scores exactly one user. User u's history is its blocks 0 to hist_blocks[u] - 1; its other blocks are unused. Some user has 16 blocks.
All inputs are finite; a program needn't handle non-finite values.
Results may differ from a plain program's by a relative error of at most 0.0054.
Values may be sent and summed in bfloat16 or wider, within the bound.
No kernel may reach another device: no remote copies, remote signals or barrier semaphores. Data moves between devices by JAX's collectives and lax.ppermute only.
A program may use at most 128 MiB of HBM per device.

v0:
```python
import math
import jax
import jax.numpy as jnp
from jax import lax
from jax.sharding import PartitionSpec as P

norm_eps = 1e-05


def partner(shard, axis, bit):
    return lax.ppermute(shard, axis, [(i, i ^ 1 << bit) for i in range(lax.axis_size(axis))])


def attend_blocks(queries, stacked, head_dim, live_steps):
    score_scale = 1.0 / math.sqrt(head_dim)

    def step_fn(running, item):
        step_index, key_block = item

        def compute(total):
            key_part = key_block[:, :head_dim]
            value_part = key_block[:, head_dim:]
            scores = lax.dot_general(
                queries, key_part, (((1,), (1,)), ((), ())), preferred_element_type=jnp.float32
            )
            weights = jax.nn.silu(scores * score_scale).astype(jnp.bfloat16)
            return total + jnp.dot(weights, value_part, preferred_element_type=jnp.float32)

        def keep_same(total):
            return total

        return (lax.cond(step_index < live_steps, compute, keep_same, running), None)

    initial = jnp.zeros((queries.shape[0], head_dim), jnp.float32)
    step_ids = jnp.arange(stacked.shape[0], dtype=jnp.int32)
    attended, unused = lax.scan(step_fn, initial, (step_ids, stacked))
    return attended


def body(pool, kv_cache, w_qu, w_out, norm_gain, cand_ids, ranker, hist_blocks, cache_slot):
    devices = lax.axis_size("rank")
    my_index = lax.axis_index("rank")
    slots_here, head_count, block_len, pair_width = kv_cache.shape
    head_dim = pair_width // 2
    user_count, most_blocks = cache_slot.shape
    model_width = pool.shape[1]
    cand_count = cand_ids.shape[1]
    slice_width = model_width // head_count
    qu_cols = 2 * head_dim
    my_group = my_index // head_count
    my_head = my_index % head_count
    bit_count = head_count.bit_length() - 1
    share_rows = cand_count // head_count
    user_range = jnp.arange(user_count, dtype=jnp.int32)
    group_match = ranker[None, :] == user_range[:, None]
    user_of_group = jnp.sum(jnp.where(group_match, user_range[None, :], 0), axis=1)
    my_user = jnp.sum(jnp.where(user_range == my_group, user_of_group, 0))
    block_range = jnp.arange(most_blocks, dtype=jnp.int32)
    live_blocks = block_range[None, :] < hist_blocks[:, None]
    owner_table = cache_slot // slots_here
    held_here = live_blocks & (owner_table == my_index)
    held_slot = jnp.sum(jnp.where(held_here, cache_slot % slots_here, 0), axis=1)
    held_flag = jnp.any(held_here, axis=1)
    slot_of_group = jnp.sum(jnp.where(group_match, held_slot[None, :], 0), axis=1)
    flag_of_group = jnp.any(group_match & held_flag[None, :], axis=1)
    outgoing = jnp.take(kv_cache, slot_of_group, axis=0)
    outgoing = jnp.where(flag_of_group[:, None, None, None], outgoing, jnp.zeros_like(outgoing))
    outgoing = outgoing.reshape(devices, block_len, pair_width)
    incoming = lax.all_to_all(outgoing, "rank", split_axis=0, concat_axis=0, tiled=True)
    my_ids = lax.dynamic_index_in_dim(cand_ids, my_user, 0, keepdims=False)
    whole_pool = lax.all_gather(pool, "rank", axis=0, tiled=True)
    cand_rows = jnp.take(whole_pool, my_ids, axis=0)
    w_head = lax.dynamic_slice_in_dim(w_qu, my_head * qu_cols, qu_cols, 1)
    head_qu = jax.nn.silu(jnp.dot(cand_rows, w_head, preferred_element_type=jnp.float32)).astype(
        jnp.bfloat16
    )
    x_part = lax.dynamic_slice_in_dim(cand_rows, my_head * slice_width, slice_width, 1)
    queries = head_qu[:, :head_dim]
    gate_part = head_qu[:, head_dim:]
    step_sources = min(16, devices)
    stacked = incoming.reshape(devices // step_sources, step_sources * block_len, pair_width)
    live_steps = stacked.shape[0]
    attended = attend_blocks(queries, stacked, head_dim, live_steps)
    total_width = head_count * head_dim
    carried = jnp.concatenate(
        [attended, gate_part.astype(jnp.float32), x_part.astype(jnp.float32)], axis=1
    )
    state = carried.reshape(head_count, share_rows, 1, carried.shape[1])
    for bit_index in reversed(range(bit_count)):
        half_count = state.shape[0] // 2
        lower_half = state[:half_count]
        upper_half = state[half_count:]
        upper_side = my_head >> bit_index & 1 == 1
        keeping = jnp.where(upper_side, upper_half, lower_half)
        giving = jnp.where(upper_side, lower_half, upper_half)
        received = partner(giving, "rank", bit_index)
        state = jnp.where(
            upper_side,
            jnp.concatenate([received, keeping], axis=2),
            jnp.concatenate([keeping, received], axis=2),
        )
    reversal = [
        sum(((source >> bit & 1) << bit_count - 1 - bit for bit in range(bit_count)))
        for source in range(head_count)
    ]
    ordered = state[0][:, jnp.array(reversal, dtype=jnp.int32), :]
    att_rows = ordered[:, :, :head_dim].reshape(share_rows, total_width)
    gate_rows = ordered[:, :, head_dim:qu_cols].reshape(share_rows, total_width)
    x_rows = ordered[:, :, qu_cols:].reshape(share_rows, model_width)
    mean_value = jnp.mean(att_rows, axis=1, keepdims=True)
    variance = jnp.mean(att_rows * att_rows, axis=1, keepdims=True) - mean_value * mean_value
    hidden = (
        (att_rows - mean_value) * lax.rsqrt(variance + norm_eps) * norm_gain[None, :] * gate_rows
    ).astype(jnp.bfloat16)
    my_rows = x_rows + jnp.dot(hidden, w_out, preferred_element_type=jnp.float32)
    return my_rows.astype(jnp.bfloat16)


def solution(mesh):
    in_specs = (
        P(("groups", "rank"), None),
        P(("groups", "rank"), None, None, None),
        P(),
        P(),
        P(),
        P("groups", None),
        P(),
        P("groups"),
        P("groups", None),
    )
    out_specs = P(("groups", "rank"), None)
    return jax.shard_map(body, mesh=mesh, in_specs=in_specs, out_specs=out_specs, check_vma=False)
```

profile of v0, /device:TPU:0, one launch (start us, length us, event | category | flops | bytes accessed | tf_op | source)
XLA Modules:
  0.0 151.2 jit_solution(3385824127241586557)
XLA Ops:
  0.0 1.0 fusion.26
  1.0 0.8 fusion.16
  1.8 0.8 select_reduce_fusion
  2.8 0.8 fusion.18
  3.8 1.6 %gather_fusion.1 = bf16[4,4,64,256]{3,2,1,0:T(8,128)(2,1)S(1)} fusion(bf16[4,4,64,256]{3,2,1,0:T(8,128)(2,1)} %param.11, s32[1024]{0:T(1024)S(1)} %pad_clamp_fusion.1), kind=kCustom, calls=%fused_computation.1 | custom fusion | bytes 1048592 | tf_op jit(solution)/shard_map/jit(_take)/gather | solution.py:66
  5.4 1.0 fusion.6
  6.4 7.4 %all-to-all-start = ((bf16[16,64,256]{2,1,0:T(8,128)(2,1)}), bf16[16,64,256]{2,1,0:T(8,128)(2,1)}, u32[]{:S(2)}, u32[]{:S(2)}) async-start(bf16[16,64,256]{2,1,0:T(8,128)(2,1)} %fusion.6), calls=%async_computation | async-start | bytes 1048576 | tf_op jit(solution)/shard_map/all_to_all | solution.py:69
  13.8 0.6 fusion.22
  16.4 0.8 compare_select_fusion
  17.2 23.5 %all_gather.3 = bf16[256,1024]{1,0:T(8,128)(2,1)S(1)} all-gather(bf16[16,1024]{1,0:T(8,128)(2,1)} %param.10), channel_id=1, replica_groups=mesh['groups'=2,'rank'=16] {'rank'}, dimensions={0}, use_global_device_ids=true | all-gather | bytes 557056 | tf_op jit(solution)/shard_map/all_gather | solution.py:71
  40.7 9.7 %gather_fusion = bf16[2048,1024]{1,0:T(8,128)(2,1)} fusion(bf16[256,1024]{1,0:T(8,128)(2,1)S(1)} %all_gather.3, s32[2048]{0:T(1024)S(1)} %broadcast_clamp_fusion), kind=kCustom, calls=%fused_computation | custom fusion | bytes 8396800 | tf_op jit(solution)/shard_map/jit(_take)/gather | solution.py:72
  50.3 3.8 %broadcast_select_fusion = bf16[2048,1024]{1,0:T(8,128)(2,1)} fusion(bf16[2048,1024]{1,0:T(8,128)(2,1)} %gather_fusion, pred[2048]{0:T(1024)(128)(4,1)S(1)} %compare_and_fusion), kind=kLoop, calls=%fused_computation.7 | loop fusion | flops 2097152 | bytes 8390656 | tf_op jit(solution)/shard_map/jit(_take)/select_n | solution.py:72
  54.1 4.8 %multiply_convert_fusion.1 = bf16[2048,256]{0,1:T(8,128)(2,1)} fusion(bf16[2048,1024]{1,0:T(8,128)(2,1)} %broadcast_select_fusion, bf16[1024,1024]{1,0:T(8,128)(2,1)S(1)} %copy-done, s32[]{:T(128)S(6)} %select_n.171), kind=kOutput, calls=%fused_computation.11 | convolution fusion | flops 1076363264 | bytes 5767172 | tf_op jit(solution)/shard_map/dot_general | solution.py:74
  58.9 1.1 slice_convert_fusion
  60.0 1.3 copy.32
  61.4 2.7 %dynamic-slice_convert_fusion = f32[2048,256]{1,0:T(8,128)} fusion(bf16[2048,1024]{1,0:T(8,128)(2,1)} %broadcast_select_fusion, s32[]{:T(128)S(6)} %select_n.171), kind=kLoop, calls=%fused_computation.22 | loop fusion | flops 524288 | bytes 3145732 | tf_op jit(solution)/shard_map/convert_element_type | solution.py:86
  64.1 4.8 %fusion = f32[2048,128]{1,0:T(8,128)} fusion(bf16[2048,256]{0,1:T(8,128)(2,1)} %multiply_convert_fusion.1, bf16[1024,256]{1,0:T(8,128)(2,1)} %bitcast.6), kind=kOutput, calls=%fused_computation.15 | convolution fusion | flops 1086324736 | bytes 2097152 | tf_op jit(solution)/shard_map/while/body/eval_jaxpr/cond/branch_1_fun/dot_general | solution.py:27
  68.9 2.3 %pad_maximum_fusion = f32[2048,512]{1,0:T(8,128)S(1)} fusion(f32[2048,256]{1,0:T(8,128)} %dynamic-slice_convert_fusion, f32[2048,128]{1,0:T(8,128)S(1)} %copy-done.4, f32[2048,128]{1,0:T(8,128)} %fusion), kind=kLoop, calls=%fused_computation.4 | loop fusion | flops 2097152 | bytes 8388608 | tf_op jit(solution)/shard_map/concatenate | solution.py:85
  71.2 2.4 %slice_select_fusion.2 = (f32[1024,512]{1,0:T(8,128)}, f32[1024,512]{1,0:T(8,128)}) fusion(f32[2048,512]{1,0:T(8,128)S(1)} %pad_maximum_fusion, pred[]{:T(512)S(6)} %eq.36), kind=kLoop, calls=%fused_computation.14 | loop fusion | flops 1048576 | bytes 8388609 | tf_op jit(solution)/shard_map/jit(_where)/select_n | solution.py:95
  73.6 1.4 collective-permute-start
  75.0 46.8 %collective-permute-done = f32[2,512,1,512]{3,1,2,0:T(8,128)} collective-permute-done((f32[2,512,1,512]{3,1,2,0:T(8,128)}, f32[2,512,1,512]{3,1,2,0:T(8,128)}, u32[]{:S(2)}, u32[]{:S(2)}) %collective-permute-start) | collective-permute-done | bytes 2097184 | tf_op jit(solution)/shard_map/ppermute | solution.py:11
  121.8 4.5 %maximum_select_fusion = f32[2,512,2,512]{3,1,2,0:T(8,128)S(1)} fusion(f32[2,512,1,512]{3,1,2,0:T(8,128)} %bitcast.45, f32[2,512,1,512]{3,1,2,0:T(8,128)} %collective-permute-done, pred[]{:T(512)S(6)} %eq.36), kind=kLoop, calls=%fused_computation.5 | loop fusion | flops 3145728 | bytes 8388609 | tf_op jit(solution)/shard_map/jit(_where)/select_n | solution.py:97
  126.4 0.5 slice_select_fusion
  127.0 4.1 %collective-permute-done.1 = f32[1,512,2,512]{3,1,2,0:T(8,128)S(1)} collective-permute-done((f32[1,512,2,512]{3,1,2,0:T(8,128)S(1)}, f32[1,512,2,512]{3,1,2,0:T(8,128)S(1)}, u32[]{:S(2)}, u32[]{:S(2)}) %collective-permute-start.1) | collective-permute-done | bytes 2097184 | tf_op jit(solution)/shard_map/ppermute | solution.py:11
  131.1 2.5 %maximum_select_fusion.1 = f32[512,4,512]{2,0,1:T(8,128)} fusion(f32[512,2,512]{2,0,1:T(8,128)S(1)} %get-tuple-element.37, f32[512,2,512]{2,0,1:T(8,128)S(1)} %bitcast.46, pred[]{:T(512)S(6)} %eq.35), kind=kLoop, calls=%fused_computation.6 | loop fusion | flops 3145728 | bytes 8388609 | tf_op jit(solution)/shard_map/jit(_where)/select_n | solution.py:97
  133.5 5.0 %gather_fusion.2 = f32[4,512,512]{2,1,0:T(8,128)} fusion(f32[512,4,512]{2,0,1:T(8,128)} %maximum_select_fusion.1, s32[1024]{0:T(1024)S(1)} %pad_clamp_fusion), kind=kCustom, calls=%fused_computation.2 | custom fusion | bytes 8388624 | tf_op jit(solution)/shard_map/gather | solution.py:106
  138.5 2.8 %slice_reduce_fusion = (f32[512]{0:T(512)S(1)}, f32[512]{0:T(512)S(1)}, f32[512,4,128]{2,0,1:T(8,128)}, f32[512,4,128]{2,0,1:T(8,128)S(1)}) fusion(f32[512,4,512]{2,0,1:T(8,128)} %bitcast.42), kind=kLoop, calls=%fused_computation.67 | loop fusion | flops 785408 | bytes 4198400 | tf_op jit(solution)/shard_map/reduce_sum | solution.py:110
  141.6 1.6 %slice_bitcast_fusion = f32[4,64,8,256]{3,2,1,0:T(8,128)} fusion(f32[512,4,512]{2,0,1:T(8,128)S(1)} %bitcast.43), kind=kLoop, calls=%fused_computation.8 | loop fusion | bytes 4194304
  143.2 2.6 %copy.37 = f32[512,4,128]{0,2,1:T(8,128)} copy(f32[512,4,128]{2,0,1:T(8,128)} %get-tuple-element.34) | data formatting | bytes 2097152 | tf_op jit(solution)/shard_map/slice | solution.py:107
  145.7 1.3 copy.38
  147.0 2.0 %copy.40 = f32[4,64,8,256]{3,2,0,1:T(8,128)S(1)} copy(f32[4,64,8,256]{3,2,1,0:T(8,128)} %slice_bitcast_fusion) | data formatting | bytes 4194304 | tf_op jit(solution)/shard_map/reshape | solution.py:109
  149.5 1.7 %add_convert_fusion = bf16[512,1024]{1,0:T(8,128)(2,1)} fusion(f32[512,1024]{1,0:T(8,128)S(1)} %bitcast.44, bf16[512,512]{0,1:T(8,128)(2,1)S(1)} %fusion.1, bf16[512,1024]{1,0:T(8,128)(2,1)S(1)} %copy-done.5), kind=kOutput, calls=%fused_computation.9 | convolution fusion | flops 537919488 | bytes 4718592 | tf_op jit(solution)/shard_map/dot_general | solution.py:115
  (30 shorter events, 1.2 us)
Async XLA Ops:
  0.0 54.1 %copy-start = (bf16[1024,1024]{1,0:T(8,128)(2,1)S(1)}, bf16[1024,1024]{1,0:T(8,128)(2,1)}, u32[]{:S(2)}) copy-start(bf16[1024,1024]{1,0:T(8,128)(2,1)} %param.12) | copy-start | bytes 6291460
  6.4 57.7 %all-to-all-start = ((bf16[16,64,256]{2,1,0:T(8,128)(2,1)}), bf16[16,64,256]{2,1,0:T(8,128)(2,1)}, u32[]{:S(2)}, u32[]{:S(2)}) async-start(bf16[16,64,256]{2,1,0:T(8,128)(2,1)} %fusion.6), calls=%async_computation | async-start | bytes 1048576 | tf_op jit(solution)/shard_map/all_to_all | solution.py:69
  64.1 4.8 %copy-start.4 = (f32[2048,128]{1,0:T(8,128)S(1)}, f32[2048,128]{1,0:T(8,128)}, u32[]{:S(2)}) copy-start(f32[2048,128]{1,0:T(8,128)} %copy.32) | copy-start | bytes 3145732
  73.6 48.2 %collective-permute-start = (f32[2,512,1,512]{3,1,2,0:T(8,128)}, f32[2,512,1,512]{3,1,2,0:T(8,128)}, u32[]{:S(2)}, u32[]{:S(2)}) collective-permute-start(f32[2,512,1,512]{3,1,2,0:T(8,128)} %bitcast.8), channel_id=1, source_target_pairs={{0,2},{1,3},{2,0},{3,1},{4,6},{5,7},{6,4},{7,5},{8,10},{9,11},{10,... | collective-permute-start | bytes 6291464 | tf_op jit(solution)/shard_map/ppermute | solution.py:11
  126.3 0.7 copy-start.7
  126.9 4.2 %collective-permute-start.1 = (f32[1,512,2,512]{3,1,2,0:T(8,128)S(1)}, f32[1,512,2,512]{3,1,2,0:T(8,128)S(1)}, u32[]{:S(2)}, u32[]{:S(2)}) collective-permute-start(f32[1,512,2,512]{3,1,2,0:T(8,128)S(1)} %get-tuple-element.36), channel_id=1, source_target_pairs={{0,1},{1,0},{2,3},{3,2},{4,5},{5,4},{6,7},{7,6},{8,9},{9,8},{10,11... | collective-permute-start | bytes 6291464 | tf_op jit(solution)/shard_map/ppermute | solution.py:11
  138.5 3.0 %copy-start.1 = (f32[4,512,512]{2,1,0:T(8,128)S(1)}, f32[4,512,512]{2,1,0:T(8,128)}, u32[]{:S(2)}) copy-start(f32[4,512,512]{2,1,0:T(8,128)} %gather_fusion.2) | copy-start | bytes 12582916
  143.2 5.9 %copy-start.6 = (f32[512]{0:T(512)S(1)}, f32[512]{0:T(512)}, u32[]{:S(2)}) copy-start(f32[512]{0:T(512)} %param.14) | copy-start | bytes 6148
  147.0 2.0 %copy-start.2 = (f32[512,4,128]{0,2,1:T(8,128)S(1)}, f32[512,4,128]{0,2,1:T(8,128)}, u32[]{:S(2)}) copy-start(f32[512,4,128]{0,2,1:T(8,128)} %copy.37) | copy-start | bytes 3145732
  147.0 2.2 %copy-start.3 = (f32[512,4,128]{0,2,1:T(8,128)S(1)}, f32[512,4,128]{0,2,1:T(8,128)}, u32[]{:S(2)}) copy-start(f32[512,4,128]{0,2,1:T(8,128)} %copy.38) | copy-start | bytes 3145732
  147.0 2.5 %copy-start.5 = (bf16[512,1024]{1,0:T(8,128)(2,1)S(1)}, bf16[512,1024]{1,0:T(8,128)(2,1)}, u32[]{:S(2)}) copy-start(bf16[512,1024]{1,0:T(8,128)(2,1)} %param.13) | copy-start | bytes 3145732
where the time goes:
time: 152 us; the launch traced here: 151 us
  waiting for transfers between devices  50.9 us (33%)
  other arithmetic  28.6 us (19%)
  local copies, waits for them, and re-layouts  25.9 us (17%)
  blocking collectives  23.5 us (15%)
  matrix products  11.3 us (7%)
  starting transfers between devices  8.88 us (6%)
  between operations  2.11 us (1%)
    ppermute x2, waiting for transfers between devices, partner(): lax.ppermute(shard, axis, [(i, i ^ 1 << bit) for i in range(lax.axis_size...  50.9 us
    all_gather x1, blocking collectives, body(): whole_pool = lax.all_gather(pool, 'rank', axis=0, tiled=True)  23.5 us
    gather x1, local copies, waits for them, and re-layouts, body(): cand_rows = jnp.take(whole_pool, my_ids, axis=0)  9.66 us
    all_to_all x1, starting transfers between devices, body(): lax.all_to_all(outgoing, 'rank', split_axis=0, concat_axis=0, tiled=True)  7.44 us
    select_n x2, other arithmetic, body(): jnp.where(upper_side, jnp.concatenate([received, keeping], axis=2), jnp.c...  6.96 us
    gather x1, local copies, waits for them, and re-layouts, body(): ordered = state[0][:, jnp.array(reversal, dtype=jnp.int32), :]  4.97 us
    dot_general x1, matrix products, compute(): jnp.dot(weights, value_part, preferred_element_type=jnp.float32)  4.83 us
    dot_general x1, matrix products, body(): jnp.dot(cand_rows, w_head, preferred_element_type=jnp.float32)  4.77 us
  transfers between devices with their start and end apart: 3, of which 2 were waited for; matrix products, arithmetic and copies ran while one was open for 16% of the time, Pallas kernels for 0%

commit v1 on v0

--- a/solution.py
+++ b/solution.py
@@ -68,7 +68,13 @@
     outgoing = outgoing.reshape(devices, block_len, pair_width)
     incoming = lax.all_to_all(outgoing, "rank", split_axis=0, concat_axis=0, tiled=True)
     my_ids = lax.dynamic_index_in_dim(cand_ids, my_user, 0, keepdims=False)
-    whole_pool = lax.all_gather(pool, "rank", axis=0, tiled=True)
+    whole_pool = lax.all_to_all(
+        jnp.concatenate(tuple((pool for _ in range(lax.axis_size("rank")))), axis=0),
+        "rank",
+        0,
+        0,
+        tiled=True,
+    )
     cand_rows = jnp.take(whole_pool, my_ids, axis=0)
     w_head = lax.dynamic_slice_in_dim(w_qu, my_head * qu_cols, qu_cols, 1)
     head_qu = jax.nn.silu(jnp.dot(cand_rows, w_head, preferred_element_type=jnp.float32)).astype(

time: 152 us -> 155 us (1.020)
  blocking collectives: 23.5 us -> 0 us
  local copies, waits for them, and re-layouts: 25.9 us -> 49 us
  starting transfers between devices: 8.88 us -> 13.6 us
  waiting for transfers between devices: 50.9 us -> 54.8 us
  matrix products: 11.3 us -> 8.05 us
  other arithmetic: 28.6 us -> 25.4 us
    all_gather x1 -> x0, blocking collectives: 23.5 us -> none  [body(): whole_pool = lax.all_gather(pool, 'rank', axis=0, tiled=True)]
    unnamed x17 -> x32, local copies, waits for them, and re-layouts: 2.16 us -> 23.9 us
    all_to_all x0 -> x1, starting transfers between devices: none -> 7.39 us  [body(): lax.all_to_all(jnp.concatenate(tuple((pool for _ in range(lax.axis_size('...]
    all_to_all x0 -> x1, waiting for transfers between devices: none -> 4.39 us  [body(): lax.all_to_all(jnp.concatenate(tuple((pool for _ in range(lax.axis_size('...]
    all_to_all x1, starting transfers between devices: 7.44 us -> 4.24 us  [body(): lax.all_to_all(outgoing, 'rank', split_axis=0, concat_axis=0, tiled=True)]
    dot_general x1, matrix products: 4.77 us -> 1.6 us  [body(): jnp.dot(cand_rows, w_head, preferred_element_type=jnp.float32)]
  transfers between devices with their start and end apart: 3 -> 4, of which waited for: 2 -> 3; matrix products, arithmetic and copies ran while one was open for 16% -> 15% of each run, Pallas kernels for 0% -> 0%
where the time goes in v1:
time: 155 us; the launch traced here: 153 us
  waiting for transfers between devices  54.8 us (35%)
  local copies, waits for them, and re-layouts  49 us (32%)
  other arithmetic  25.4 us (16%)
  starting transfers between devices  13.6 us (9%)
  matrix products  8.05 us (5%)
  between operations  2.32 us (1%)
    ppermute x2, waiting for transfers between devices, partner(): lax.ppermute(shard, axis, [(i, i ^ 1 << bit) for i in range(lax.axis_size...  50.4 us
    unnamed x32, local copies, waits for them, and re-layouts  23.9 us
    gather x1, local copies, waits for them, and re-layouts, body(): cand_rows = jnp.take(whole_pool, my_ids, axis=0)  9.67 us
    all_to_all x1, starting transfers between devices, body(): lax.all_to_all(jnp.concatenate(tuple((pool for _ in range(lax.axis_size('...  7.39 us
    select_n x2, other arithmetic, body(): jnp.where(upper_side, jnp.concatenate([received, keeping], axis=2), jnp.c...  6.96 us
    gather x1, local copies, waits for them, and re-layouts, body(): ordered = state[0][:, jnp.array(reversal, dtype=jnp.int32), :]  4.97 us
    dot_general x1, matrix products, compute(): jnp.dot(weights, value_part, preferred_element_type=jnp.float32)  4.74 us
    all_to_all x1, waiting for transfers between devices, body(): lax.all_to_all(jnp.concatenate(tuple((pool for _ in range(lax.axis_size('...  4.39 us
  transfers between devices with their start and end apart: 4, of which 3 were waited for; matrix products, arithmetic and copies ran while one was open for 15% of the time, Pallas kernels for 0%

profile of v1, /device:TPU:0, one launch (start us, length us, event | category | flops | bytes accessed | tf_op | source)
XLA Modules:
  0.0 153.2 jit_solution(2008306571835859848)
XLA Ops:
  0.0 1.5 constant_dynamic-update-slice_fusion.15
  1.5 1.4 constant_dynamic-update-slice_fusion.14
  2.9 1.4 constant_dynamic-update-slice_fusion.13
  4.3 1.4 constant_dynamic-update-slice_fusion.12
  5.6 1.4 constant_dynamic-update-slice_fusion.11
  7.0 1.4 constant_dynamic-update-slice_fusion.10
  8.4 1.4 constant_dynamic-update-slice_fusion.9
  9.8 1.4 constant_dynamic-update-slice_fusion.8
  11.1 1.4 constant_dynamic-update-slice_fusion.7
  12.5 1.4 constant_dynamic-update-slice_fusion.6
  22.1 7.4 %all-to-all-start = ((bf16[16,16,1024]{2,1,0:T(8,128)(2,1)}), bf16[16,16,1024]{2,1,0:T(8,128)(2,1)S(1)}, u32[]{:S(2)}, u32[]{:S(2)}) async-start(bf16[16,16,1024]{2,1,0:T(8,128)(2,1)} %bitcast.1), calls=%async_computation | async-start | bytes 1048576 | tf_op jit(solution)/shard_map/all_to_all | solution.py:71
  36.0 1.6 %gather_fusion.1 = bf16[4,4,64,256]{3,2,1,0:T(8,128)(2,1)S(1)} fusion(bf16[4,4,64,256]{3,2,1,0:T(8,128)(2,1)} %param.11, s32[1024]{0:T(1024)S(1)} %pad_clamp_fusion.1), kind=kCustom, calls=%fused_computation.1 | custom fusion | bytes 1048592 | tf_op jit(solution)/shard_map/jit(_take)/gather | solution.py:66
  39.4 4.4 %all-to-all-done = bf16[16,16,1024]{2,1,0:T(8,128)(2,1)S(1)} async-done(((bf16[16,16,1024]{2,1,0:T(8,128)(2,1)}), bf16[16,16,1024]{2,1,0:T(8,128)(2,1)S(1)}, u32[]{:S(2)}, u32[]{:S(2)}) %all-to-all-start) | async-done | bytes 524320 | tf_op jit(solution)/shard_map/all_to_all | solution.py:71
  43.8 4.2 %all-to-all-start.1 = ((bf16[16,64,256]{2,1,0:T(8,128)(2,1)}), bf16[16,64,256]{2,1,0:T(8,128)(2,1)}, u32[]{:S(2)}, u32[]{:S(2)}) async-start(bf16[16,64,256]{2,1,0:T(8,128)(2,1)} %fusion.6), calls=%async_computation.1 | async-start | bytes 1048576 | tf_op jit(solution)/shard_map/all_to_all | solution.py:69
  48.1 9.7 %gather_fusion = bf16[2048,1024]{1,0:T(8,128)(2,1)} fusion(bf16[256,1024]{1,0:T(8,128)(2,1)S(1)} %bitcast.44, s32[2048]{0:T(1024)S(1)} %broadcast_clamp_fusion), kind=kCustom, calls=%fused_computation | custom fusion | bytes 8396800 | tf_op jit(solution)/shard_map/jit(_take)/gather | solution.py:78
  57.7 2.5 %broadcast_select_fusion = bf16[2048,1024]{1,0:T(8,128)(2,1)S(1)} fusion(bf16[2048,1024]{1,0:T(8,128)(2,1)} %gather_fusion, pred[2048]{0:T(1024)(128)(4,1)S(1)} %compare_and_fusion), kind=kLoop, calls=%fused_computation.7 | loop fusion | flops 2097152 | bytes 8390656 | tf_op jit(solution)/shard_map/jit(_take)/select_n | solution.py:78
  60.2 1.6 %dynamic-slice_convert_fusion = f32[2048,256]{1,0:T(8,128)} fusion(bf16[2048,1024]{1,0:T(8,128)(2,1)S(1)} %broadcast_select_fusion, s32[]{:T(128)S(6)} %select_n.171), kind=kLoop, calls=%fused_computation.22 | loop fusion | flops 524288 | bytes 3145732 | tf_op jit(solution)/shard_map/convert_element_type | solution.py:92
  61.8 1.6 %multiply_convert_fusion.1 = bf16[2048,256]{0,1:T(8,128)(2,1)S(1)} fusion(bf16[2048,1024]{1,0:T(8,128)(2,1)S(1)} %broadcast_select_fusion, bf16[1024,1024]{1,0:T(8,128)(2,1)S(1)} %copy-done, s32[]{:T(128)S(6)} %select_n.171), kind=kOutput, calls=%fused_computation.11 | convolution fusion | flops 1076363264 | bytes 5767172 | tf_op jit(solution)/shard_map/dot_general | solution.py:80
  64.5 4.7 %fusion = f32[2048,128]{1,0:T(8,128)} fusion(bf16[2048,256]{0,1:T(8,128)(2,1)} %copy-done.5, bf16[1024,256]{1,0:T(8,128)(2,1)} %bitcast.8), kind=kOutput, calls=%fused_computation.15 | convolution fusion | flops 1086324736 | bytes 2097152 | tf_op jit(solution)/shard_map/while/body/eval_jaxpr/cond/branch_1_fun/dot_general | solution.py:27
  70.6 2.6 %pad_maximum_fusion = f32[2048,512]{1,0:T(8,128)S(1)} fusion(f32[2048,256]{1,0:T(8,128)} %dynamic-slice_convert_fusion, f32[2048,128]{1,0:T(8,128)} %copy.32, f32[2048,128]{1,0:T(8,128)} %fusion), kind=kLoop, calls=%fused_computation.4 | loop fusion | flops 2097152 | bytes 8388608 | tf_op jit(solution)/shard_map/concatenate | solution.py:91
  73.1 2.4 %slice_select_fusion.2 = (f32[1024,512]{1,0:T(8,128)}, f32[1024,512]{1,0:T(8,128)}) fusion(f32[2048,512]{1,0:T(8,128)S(1)} %pad_maximum_fusion, pred[]{:T(512)S(6)} %eq.36), kind=kLoop, calls=%fused_computation.14 | loop fusion | flops 1048576 | bytes 8388609 | tf_op jit(solution)/shard_map/jit(_where)/select_n | solution.py:101
  75.6 1.9 %collective-permute-start = (f32[2,512,1,512]{3,1,2,0:T(8,128)}, f32[2,512,1,512]{3,1,2,0:T(8,128)}, u32[]{:S(2)}, u32[]{:S(2)}) collective-permute-start(f32[2,512,1,512]{3,1,2,0:T(8,128)} %bitcast.10), channel_id=1, source_target_pairs={{0,2},{1,3},{2,0},{3,1},{4,6},{5,7},{6,4},{7,5},{8,10},{9,11},{10,... | collective-permute-start | bytes 6291464 | tf_op jit(solution)/shard_map/ppermute | solution.py:11
  77.5 46.3 %collective-permute-done = f32[2,512,1,512]{3,1,2,0:T(8,128)} collective-permute-done((f32[2,512,1,512]{3,1,2,0:T(8,128)}, f32[2,512,1,512]{3,1,2,0:T(8,128)}, u32[]{:S(2)}, u32[]{:S(2)}) %collective-permute-start) | collective-permute-done | bytes 2097184 | tf_op jit(solution)/shard_map/ppermute | solution.py:11
  123.8 4.5 %maximum_select_fusion = f32[2,512,2,512]{3,1,2,0:T(8,128)S(1)} fusion(f32[2,512,1,512]{3,1,2,0:T(8,128)} %bitcast.48, f32[2,512,1,512]{3,1,2,0:T(8,128)} %collective-permute-done, pred[]{:T(512)S(6)} %eq.36), kind=kLoop, calls=%fused_computation.5 | loop fusion | flops 3145728 | bytes 8388609 | tf_op jit(solution)/shard_map/jit(_where)/select_n | solution.py:103
  129.0 4.1 %collective-permute-done.1 = f32[1,512,2,512]{3,1,2,0:T(8,128)S(1)} collective-permute-done((f32[1,512,2,512]{3,1,2,0:T(8,128)S(1)}, f32[1,512,2,512]{3,1,2,0:T(8,128)S(1)}, u32[]{:S(2)}, u32[]{:S(2)}) %collective-permute-start.1) | collective-permute-done | bytes 2097184 | tf_op jit(solution)/shard_map/ppermute | solution.py:11
  133.1 2.5 %maximum_select_fusion.1 = f32[512,4,512]{2,0,1:T(8,128)} fusion(f32[512,2,512]{2,0,1:T(8,128)S(1)} %get-tuple-element.37, f32[512,2,512]{2,0,1:T(8,128)S(1)} %bitcast.49, pred[]{:T(512)S(6)} %eq.35), kind=kLoop, calls=%fused_computation.6 | loop fusion | flops 3145728 | bytes 8388609 | tf_op jit(solution)/shard_map/jit(_where)/select_n | solution.py:103
  135.5 5.0 %gather_fusion.2 = f32[4,512,512]{2,1,0:T(8,128)} fusion(f32[512,4,512]{2,0,1:T(8,128)} %maximum_select_fusion.1, s32[1024]{0:T(1024)S(1)} %pad_clamp_fusion), kind=kCustom, calls=%fused_computation.2 | custom fusion | bytes 8388624 | tf_op jit(solution)/shard_map/gather | solution.py:112
  140.5 2.8 %slice_reduce_fusion = (f32[512]{0:T(512)S(1)}, f32[512]{0:T(512)S(1)}, f32[512,4,128]{2,0,1:T(8,128)}, f32[512,4,128]{2,0,1:T(8,128)S(1)}) fusion(f32[512,4,512]{2,0,1:T(8,128)} %bitcast.45), kind=kLoop, calls=%fused_computation.83 | loop fusion | flops 785408 | bytes 4198400 | tf_op jit(solution)/shard_map/reduce_sum | solution.py:116
  143.5 1.6 %slice_bitcast_fusion = f32[4,64,8,256]{3,2,1,0:T(8,128)} fusion(f32[512,4,512]{2,0,1:T(8,128)S(1)} %bitcast.46), kind=kLoop, calls=%fused_computation.8 | loop fusion | bytes 4194304
  145.1 2.6 %copy.37 = f32[512,4,128]{0,2,1:T(8,128)} copy(f32[512,4,128]{2,0,1:T(8,128)} %get-tuple-element.34) | data formatting | bytes 2097152 | tf_op jit(solution)/shard_map/slice | solution.py:113
  149.0 2.0 %copy.40 = f32[4,64,8,256]{3,2,0,1:T(8,128)S(1)} copy(f32[4,64,8,256]{3,2,1,0:T(8,128)} %slice_bitcast_fusion) | data formatting | bytes 4194304 | tf_op jit(solution)/shard_map/reshape | solution.py:115
  151.5 1.7 %add_convert_fusion = bf16[512,1024]{1,0:T(8,128)(2,1)} fusion(f32[512,1024]{1,0:T(8,128)S(1)} %bitcast.47, bf16[512,512]{0,1:T(8,128)(2,1)S(1)} %fusion.1, bf16[512,1024]{1,0:T(8,128)(2,1)S(1)} %copy-done.4), kind=kOutput, calls=%fused_computation.9 | convolution fusion | flops 537919488 | bytes 4718592 | tf_op jit(solution)/shard_map/dot_general | solution.py:121
  (47 shorter events, 19.3 us)
Async XLA Ops:
  0.0 61.8 %copy-start = (bf16[1024,1024]{1,0:T(8,128)(2,1)S(1)}, bf16[1024,1024]{1,0:T(8,128)(2,1)}, u32[]{:S(2)}) copy-start(bf16[1024,1024]{1,0:T(8,128)(2,1)} %param.12) | copy-start | bytes 6291460
  22.1 21.7 %all-to-all-start = ((bf16[16,16,1024]{2,1,0:T(8,128)(2,1)}), bf16[16,16,1024]{2,1,0:T(8,128)(2,1)S(1)}, u32[]{:S(2)}, u32[]{:S(2)}) async-start(bf16[16,16,1024]{2,1,0:T(8,128)(2,1)} %bitcast.1), calls=%async_computation | async-start | bytes 1048576 | tf_op jit(solution)/shard_map/all_to_all | solution.py:71
  43.8 20.7 %all-to-all-start.1 = ((bf16[16,64,256]{2,1,0:T(8,128)(2,1)}), bf16[16,64,256]{2,1,0:T(8,128)(2,1)}, u32[]{:S(2)}, u32[]{:S(2)}) async-start(bf16[16,64,256]{2,1,0:T(8,128)(2,1)} %fusion.6), calls=%async_computation.1 | async-start | bytes 1048576 | tf_op jit(solution)/shard_map/all_to_all | solution.py:69
  63.4 1.0 copy-start.5
  75.6 48.2 %collective-permute-start = (f32[2,512,1,512]{3,1,2,0:T(8,128)}, f32[2,512,1,512]{3,1,2,0:T(8,128)}, u32[]{:S(2)}, u32[]{:S(2)}) collective-permute-start(f32[2,512,1,512]{3,1,2,0:T(8,128)} %bitcast.10), channel_id=1, source_target_pairs={{0,2},{1,3},{2,0},{3,1},{4,6},{5,7},{6,4},{7,5},{8,10},{9,11},{10,... | collective-permute-start | bytes 6291464 | tf_op jit(solution)/shard_map/ppermute | solution.py:11
  128.3 0.7 copy-start.7
  128.8 4.2 %collective-permute-start.1 = (f32[1,512,2,512]{3,1,2,0:T(8,128)S(1)}, f32[1,512,2,512]{3,1,2,0:T(8,128)S(1)}, u32[]{:S(2)}, u32[]{:S(2)}) collective-permute-start(f32[1,512,2,512]{3,1,2,0:T(8,128)S(1)} %get-tuple-element.36), channel_id=1, source_target_pairs={{0,1},{1,0},{2,3},{3,2},{4,5},{5,4},{6,7},{7,6},{8,9},{9,8},{10,11... | collective-permute-start | bytes 6291464 | tf_op jit(solution)/shard_map/ppermute | solution.py:11
  140.5 3.0 %copy-start.1 = (f32[4,512,512]{2,1,0:T(8,128)S(1)}, f32[4,512,512]{2,1,0:T(8,128)}, u32[]{:S(2)}) copy-start(f32[4,512,512]{2,1,0:T(8,128)} %gather_fusion.2) | copy-start | bytes 12582916
  145.1 5.9 %copy-start.6 = (f32[512]{0:T(512)S(1)}, f32[512]{0:T(512)}, u32[]{:S(2)}) copy-start(f32[512]{0:T(512)} %param.14) | copy-start | bytes 6148
  149.0 2.0 %copy-start.2 = (f32[512,4,128]{0,2,1:T(8,128)S(1)}, f32[512,4,128]{0,2,1:T(8,128)}, u32[]{:S(2)}) copy-start(f32[512,4,128]{0,2,1:T(8,128)} %copy.37) | copy-start | bytes 3145732
  149.0 2.2 %copy-start.3 = (f32[512,4,128]{0,2,1:T(8,128)S(1)}, f32[512,4,128]{0,2,1:T(8,128)}, u32[]{:S(2)}) copy-start(f32[512,4,128]{0,2,1:T(8,128)} %copy.38) | copy-start | bytes 3145732
  149.0 2.5 %copy-start.4 = (bf16[512,1024]{1,0:T(8,128)(2,1)S(1)}, bf16[512,1024]{1,0:T(8,128)(2,1)}, u32[]{:S(2)}) copy-start(bf16[512,1024]{1,0:T(8,128)(2,1)} %param.13) | copy-start | bytes 3145732
